TPU v7x, 32 devices: a whole 2x2x4 slice. The times are simulated.
32 devices in a mesh: groups: 2 (over y), tok: 4 (over z), ch: 2 (over x), sub: 2 (over core).
Axes of the slice: x: 2, y: 2, z: 4, core: 2. Of those that a mesh axis runs over, the one named last changes fastest.
Arguments:
- weather: float32 [128, 128, 128], P('groups', 'tok', ('ch', 'sub')), parts along dimension 0, may hold values from -6 to 6
- conv_first: float32 [9, 64, 64], replicated, may hold values from -0.25 to 0.25
- conv_second: float32 [9, 64, 64], replicated, may hold values from -0.25 to 0.25
- patch_embed: bfloat16 [256, 384], replicated, may hold values from -0.375 to 0.375
- token_mixing: bfloat16 [4096, 16384], P('tok', ('ch', 'sub')), may hold values from -0.09375 to 0.09375
Outputs:
- lifted: bfloat16 [768, 16384], P(('groups', 'tok'), ('ch', 'sub')), parts along dimension 0
There are 2 independent parts, one for each index of `groups`. A program takes and returns all parts, laid end to end along the dimension named above; an argument that names none is the same for every part. Nothing has to cross between parts.
All inputs are finite; a program needn't handle non-finite values.
Results may differ from a plain program's by a relative error of at most 0.0058.
Values may be sent and summed in bfloat16 or wider, within the bound.
A program may use at most 64 MiB of HBM per device.

v0:
```python
import jax
import jax.numpy as jnp
from jax import lax
from jax.sharding import PartitionSpec as P


def padded_2(block, sides, width, periodic):
    for axis, dim in sides:
        count = lax.axis_size(axis)
        forward = [(i, i + 1) for i in range(count - 1)]
        if periodic:
            forward.append((count - 1, 0))
        backward = [(target, source) for source, target in forward]
        low = lax.ppermute(
            lax.slice_in_dim(block, block.shape[dim] - width, None, axis=dim), axis, forward
        )
        high = lax.ppermute(lax.slice_in_dim(block, 0, width, axis=dim), axis, backward)
        block = jnp.concatenate([low, block, high], axis=dim)
    return block


def valid_conv(padded, kernel):
    width_lon = padded.shape[1] - 2
    width_lat = padded.shape[2] - 2
    stacked = jnp.stack(
        [
            padded[:, row_shift : row_shift + width_lon, col_shift : col_shift + width_lat]
            for row_shift in range(3)
            for col_shift in range(3)
        ],
        0,
    )
    return jnp.einsum("toi,tixy->oxy", kernel, stacked, precision=lax.Precision.HIGHEST)


def embed_patches(field_in, patch_embed):
    chans, width_lon, width_lat = field_in.shape
    blocks = field_in.reshape(chans, width_lon // 2, 2, width_lat // 2, 2)
    embed_four = patch_embed.reshape(chans, 2, 2, patch_embed.shape[1])
    return jnp.einsum(
        "cpaqb,cabo->pqo", blocks, embed_four, preferred_element_type=jnp.float32
    ).astype(jnp.bfloat16)


def local(weather, conv_first, conv_second, patch_embed, token_mixing):
    widened = padded_2(weather, (("tok", 1),), 2, True)
    padded = padded_2(widened, ((("ch", "sub"), 2),), 2, False)
    hidden_one = jax.nn.gelu(valid_conv(padded, conv_first), approximate=False)
    width_lat = weather.shape[2]
    lat_index = (
        jnp.arange(width_lat + 2, dtype=jnp.int32) - 1 + lax.axis_index(("ch", "sub")) * width_lat
    )
    inside = (lat_index >= 0) & (lat_index < width_lat * lax.axis_size(("ch", "sub")))
    hidden_one = jnp.where(inside[None, None, :], hidden_one, jnp.float32(0.0))
    field_two = valid_conv(hidden_one, conv_second)
    field_two = field_two.astype(jnp.bfloat16)
    local_tokens = embed_patches(field_two, patch_embed)
    gathered = lax.all_gather(local_tokens, ("ch", "sub"), axis=1, tiled=True)
    tokens = gathered.reshape(-1, gathered.shape[2])
    summed = lax.psum_scatter(
        lax.dot_general(
            tokens, token_mixing, (((0,), (0,)), ((), ())), preferred_element_type=jnp.float32
        ),
        "tok",
        scatter_dimension=0,
        tiled=True,
    )
    return jax.nn.gelu(summed, approximate=False).astype(jnp.bfloat16)


def solution(mesh):
    placed = (P("groups", "tok", ("ch", "sub")), P(), P(), P(), P("tok", ("ch", "sub")))
    return jax.shard_map(
        local,
        mesh=mesh,
        in_specs=placed,
        out_specs=P(("groups", "tok"), ("ch", "sub")),
        check_vma=False,
    )
```

profile of v0, /device:TPU:0, one launch (start us, length us, event | category | flops | bytes accessed | tf_op | source)
XLA Modules:
  0.0 174.0 jit_solution(14999862905189932922)
XLA Ops:
  6.5 0.0 copy-start
  6.5 0.0 copy-start.2
  6.5 0.0 reduce-scatter.2.cloned.1.call-start
  6.5 0.8 fusion.64
  7.4 3.1 %collective-permute-start = (f32[64,2,32]{0,2,1:T(8,128)S(1)}, f32[64,2,32]{0,2,1:T(8,128)S(1)}, u32[]{:S(2)}, u32[]{:S(2)}) collective-permute-start(f32[64,2,32]{0,2,1:T(8,128)S(1)} %get-tuple-element.8), channel_id=1, source_target_pairs={{0,4},{4,8},{8,12},{12,0},{1,5},{5,9},{9,13},{13,1},{2,6},{6,10},{... | collective-permute-start | bytes 49160 | tf_op jit(solution)/shard_map/ppermute | solution.py:14
  10.4 2.1 %collective-permute-start.1 = (f32[64,2,32]{0,2,1:T(8,128)S(1)}, f32[64,2,32]{0,2,1:T(8,128)S(1)}, u32[]{:S(2)}, u32[]{:S(2)}) collective-permute-start(f32[64,2,32]{0,2,1:T(8,128)S(1)} %get-tuple-element.7), channel_id=1, source_target_pairs={{4,0},{8,4},{12,8},{0,12},{5,1},{9,5},{13,9},{1,13},{6,2},{10,6},{... | collective-permute-start | bytes 49160 | tf_op jit(solution)/shard_map/ppermute | solution.py:17
  12.5 1.9 %collective-permute-done = f32[64,2,32]{0,2,1:T(8,128)S(1)} collective-permute-done((f32[64,2,32]{0,2,1:T(8,128)S(1)}, f32[64,2,32]{0,2,1:T(8,128)S(1)}, u32[]{:S(2)}, u32[]{:S(2)}) %collective-permute-start) | collective-permute-done | bytes 16416 | tf_op jit(solution)/shard_map/ppermute | solution.py:14
  14.5 1.1 constant_dynamic-update-slice_fusion.1
  15.5 0.0 collective-permute-done.1
  15.6 1.3 collective-permute-start.2
  16.9 0.0 copy-done.2
  16.9 0.1 reshape.18
  17.0 1.3 collective-permute-start.3
  18.3 0.0 collective-permute-done.2
  18.3 0.1 fusion.23
  18.4 3.6 %collective-permute-done.3 = f32[64,36,2]{0,2,1:T(2,128)S(1)} collective-permute-done((f32[64,36,2]{0,2,1:T(2,128)S(1)}, f32[64,36,2]{0,2,1:T(2,128)S(1)}, u32[]{:S(2)}, u32[]{:S(2)}) %collective-permute-start.3) | collective-permute-done | bytes 18464 | tf_op jit(solution)/shard_map/ppermute | solution.py:17
  22.1 0.1 pad_maximum_fusion
  22.2 0.1 fusion.33
  22.2 0.1 fusion.17
  22.3 0.1 fusion.20
  22.4 0.1 fusion.32
  22.5 0.1 fusion.14
  22.5 0.1 fusion.31
  22.6 0.1 fusion.29
  22.7 0.1 fusion.28
  22.7 0.0 copy-done
  22.7 6.9 %fusion.26 = f32[64,34,34]{0,2,1:T(8,128)S(1)} fusion(f32[9,64,34,34]{1,3,0,2:T(8,128)S(1)} %fusion.28, pred[34]{0:T(512)(128)(4,1)S(1)} %compare_and_fusion, f32[9,64,64]{2,1,0:T(8,128)S(1)} %copy-done), kind=kOutput, calls=%fused_computation.48 | convolution fusion | flops 516186368 | bytes 3106850 | tf_op jit(solution)/shard_map/toi,tixy->oxy/dot_general | solution.py:33
  29.6 0.1 fusion.57
  29.7 0.0 slice-start
  29.7 0.1 fusion.56
  29.8 0.1 fusion.55
  29.8 0.1 fusion.54
  29.9 0.1 fusion.53
  30.0 0.1 fusion.52
  30.0 0.0 copy-start.1
  30.0 0.1 fusion.51
  30.1 0.1 fusion.50
  30.2 0.0 slice-start.1
  30.2 0.1 fusion.49
  30.3 0.9 copy-done.1
  31.2 3.9 %fusion.10 = bf16[32,32,64]{2,1,0:T(8,128)(2,1)S(1)} fusion(f32[9,64,32,32]{1,3,2,0:T(8,128)S(1)} %fusion.49, f32[9,64,64]{2,1,0:T(8,128)S(1)} %copy-done.1), kind=kOutput, calls=%fused_computation.21 | convolution fusion | flops 453050368 | bytes 2637824 | tf_op jit(solution)/shard_map/toi,tixy->oxy/dot_general | solution.py:33
  35.1 0.4 fusion.11
  35.6 9.5 %all_gather.3 = bf16[16,64,384]{2,1,0:T(8,128)(2,1)S(1)} all-gather(bf16[16,16,384]{2,1,0:T(8,128)(2,1)S(1)} %fusion.11), channel_id=1, replica_groups=mesh['groups'=2,'tok'=4,'ch'=2,'sub'=2] {'ch','sub'}, dimensions={1}, use_global_device_ids=true | all-gather | bytes 983040 | tf_op jit(solution)/shard_map/all_gather | solution.py:58
  45.1 0.0 slice-done
  45.1 0.0 slice-done.1
  45.1 5.3 %fusion.65 = f32[384,4096]{1,0:T(8,128)} fusion(bf16[1024,384]{1,0:T(8,128)(2,1)S(1)} %bitcast.187, bf16[1024,4096]{1,0:T(8,128)(2,1)S(1)} %bitcast.186), kind=kOutput, calls=%fused_computation.110 | convolution fusion | flops 3221225472 | bytes 15466496 | tf_op jit(solution)/shard_map/dot_general | solution.py:61
  50.4 0.0 reduce-scatter.2.cloned.1.call-update
  50.5 111.5 %reduce-scatter.2.cloned.1.call-done = f32[96,4096]{1,0:T(8,128)} async-done(((f32[384,4096]{1,0:T(8,128)}), f32[96,4096]{1,0:T(8,128)}) %reduce-scatter.2.cloned.1.call-update) | async-done | bytes 1572880 | tf_op jit(solution)/shard_map/reduce_scatter | solution.py:60
  162.0 5.2 %fusion.2 = bf16[96,4096]{1,0:T(8,128)(2,1)} fusion(f32[96,4096]{1,0:T(8,128)} %reduce-scatter.2.cloned.1.call-done), kind=kLoop, calls=%fused_computation.3 | loop fusion | flops 25559040 | bytes 2359296 | tf_op jit(solution)/shard_map/convert_element_type | solution.py:68
  (5 shorter events, 0.0 us)
Async XLA Ops:
  6.5 16.2 %copy-start = (f32[9,64,64]{2,1,0:T(8,128)S(1)}, f32[9,64,64]{2,1,0:T(8,128)}, u32[]{:S(2)}) copy-start(f32[9,64,64]{2,1,0:T(8,128)} %param.6) | copy-start | bytes 442372
  6.5 10.4 %copy-start.2 = (bf16[256,384]{1,0:T(8,128)(2,1)S(1)}, bf16[256,384]{1,0:T(8,128)(2,1)}, u32[]{:S(2)}) copy-start(bf16[256,384]{1,0:T(8,128)(2,1)} %param.8) | copy-start | bytes 589828
  6.5 155.4 %reduce-scatter.2.cloned.1.call-start = ((), (), s32[]{:S(2)}) async-start(), calls=%async_computation.1 | async-start | bytes 7864320 | tf_op jit(solution)/shard_map/reduce_scatter | solution.py:60
  7.4 7.1 %collective-permute-start = (f32[64,2,32]{0,2,1:T(8,128)S(1)}, f32[64,2,32]{0,2,1:T(8,128)S(1)}, u32[]{:S(2)}, u32[]{:S(2)}) collective-permute-start(f32[64,2,32]{0,2,1:T(8,128)S(1)} %get-tuple-element.8), channel_id=1, source_target_pairs={{0,4},{4,8},{8,12},{12,0},{1,5},{5,9},{9,13},{13,1},{2,6},{6,10},{... | collective-permute-start | bytes 49160 | tf_op jit(solution)/shard_map/ppermute | solution.py:14
  10.4 5.1 %collective-permute-start.1 = (f32[64,2,32]{0,2,1:T(8,128)S(1)}, f32[64,2,32]{0,2,1:T(8,128)S(1)}, u32[]{:S(2)}, u32[]{:S(2)}) collective-permute-start(f32[64,2,32]{0,2,1:T(8,128)S(1)} %get-tuple-element.7), channel_id=1, source_target_pairs={{4,0},{8,4},{12,8},{0,12},{5,1},{9,5},{13,9},{1,13},{6,2},{10,6},{... | collective-permute-start | bytes 49160 | tf_op jit(solution)/shard_map/ppermute | solution.py:17
  15.6 2.7 %collective-permute-start.2 = (f32[64,36,2]{0,2,1:T(2,128)S(1)}, f32[64,36,2]{0,2,1:T(2,128)S(1)}, u32[]{:S(2)}, u32[]{:S(2)}) collective-permute-start(f32[64,36,2]{0,2,1:T(2,128)S(1)} %get-tuple-element.6), channel_id=1, source_target_pairs={{0,1},{1,2},{2,3},{4,5},{5,6},{6,7},{8,9},{9,10},{10,11},{12,13},{... | collective-permute-start | bytes 55304 | tf_op jit(solution)/shard_map/ppermute | solution.py:14
  17.0 5.1 %collective-permute-start.3 = (f32[64,36,2]{0,2,1:T(2,128)S(1)}, f32[64,36,2]{0,2,1:T(2,128)S(1)}, u32[]{:S(2)}, u32[]{:S(2)}) collective-permute-start(f32[64,36,2]{0,2,1:T(2,128)S(1)} %get-tuple-element.5), channel_id=1, source_target_pairs={{1,0},{2,1},{3,2},{5,4},{6,5},{7,6},{9,8},{10,9},{11,10},{13,12},{... | collective-permute-start | bytes 55304 | tf_op jit(solution)/shard_map/ppermute | solution.py:17
  29.7 15.4 %slice-start = ((s8[8388608]{0:T(1024)(128)(4,1)}), s8[4194304]{0:T(1024)(128)(4,1)S(1)}, s32[]{:S(2)}) async-start(s8[8388608]{0:T(1024)(128)(4,1)} %bitcast.185), calls=%async_computation.2 | async-start | bytes 8388608
  30.0 1.1 copy-start.1
  30.2 14.9 %slice-start.1 = ((s8[8388608]{0:T(1024)(128)(4,1)}), s8[4194304]{0:T(1024)(128)(4,1)S(1)}, s32[]{:S(2)}) async-start(s8[8388608]{0:T(1024)(128)(4,1)} %bitcast.185), calls=%async_computation.3 | async-start | bytes 8388608
Sparse Core Ops, SparseCore 0:
  50.6 111.3 reduce-scatter.1
where the time goes:
time: 174 us
  waiting for transfers between devices  117 us (67%)
  matrix products  16.6 us (10%)
  between operations  13.7 us (8%)
  blocking collectives  9.54 us (5%)
  starting transfers between devices  7.72 us (4%)
  other arithmetic  5.78 us (3%)
  local copies, waits for them, and re-layouts  3.67 us (2%)
    reduce_scatter x1, waiting for transfers between devices, local(): lax.psum_scatter(lax.dot_general(tokens, token_mixing, (((0,), (0,)), (()...  111 us
    dot_general x2, matrix products, valid_conv(): jnp.einsum('toi,tixy->oxy', kernel, stacked, precision=lax.Precision.HIGH...  10.8 us
    all_gather x1, blocking collectives, local(): gathered = lax.all_gather(local_tokens, ('ch', 'sub'), axis=1, tiled=True)  9.54 us
    dot_general x1, matrix products, local(): lax.dot_general(tokens, token_mixing, (((0,), (0,)), ((), ())), preferred...  5.32 us
    convert_element_type x1, other arithmetic, local(): return jax.nn.gelu(summed, approximate=False).astype(jnp.bfloat16)  5.23 us
    ppermute x2, starting transfers between devices, padded_2(): lax.ppermute(lax.slice_in_dim(block, block.shape[dim] - width, None, axis...  4.34 us
    ppermute x2, waiting for transfers between devices, padded_2(): lax.ppermute(lax.slice_in_dim(block, 0, width, axis=dim), axis, backward)  3.65 us
  transfers between devices with their start and end apart: 5, of which 3 were waited for; matrix products, arithmetic and copies ran while one was open for 1% of the time, Pallas kernels for 0%

commit v1 on v0

--- a/solution.py
+++ b/solution.py
@@ -1,7 +1,15 @@
+import functools
+
 import jax
 import jax.numpy as jnp
 from jax import lax
+from jax.experimental import pallas as pl
+from jax.experimental.pallas import tpu as pltpu
 from jax.sharding import PartitionSpec as P
+
+MESH = pl.DeviceIdType.MESH
+CHUNKS = 8
+PIECES = 2
 
 
 def padded_2(block, sides, width, periodic):
@@ -42,6 +50,183 @@
     ).astype(jnp.bfloat16)
 
 
+def gelu_exact(v):
+    return 0.5 * v * (1.0 + lax.erf(v * 0.7071067811865476))
+
+
+def lift_kernel(
+    n, tok_ref, w_ref, out_ref, tg, tt, wv, part, s_r, s_l, r_r, r_l,
+    w_sem, ga_s, ga_r, gb_s, gb_r, gf_s, gf_r, rs_s, rs_r, ls_s, ls_r,
+):
+    z, x, s = lax.axis_index("tok"), lax.axis_index("ch"), lax.axis_index("sub")
+    chunks, _, ob, hc = s_r.shape
+    pieces = ga_s.shape[0]
+
+    def w_copy(c):
+        return pltpu.make_async_copy(
+            w_ref.at[:, pl.ds(pl.multiple_of(c * hc, hc), hc)], wv.at[c], w_sem.at[c]
+        )
+
+    for c in range(chunks):
+        w_copy(c).start()
+
+    barrier = pltpu.get_barrier_semaphore()
+    pl.semaphore_signal(barrier, inc=1, device_id={"ch": 1 - x}, device_id_type=MESH)
+    pl.semaphore_signal(barrier, inc=1, device_id={"sub": 1 - s}, device_id_type=MESH)
+
+    for peer in (lax.rem(z + 1, n), lax.rem(z + n - 1, n)):
+        pl.semaphore_signal(barrier, inc=1, device_id={"tok": peer}, device_id_type=MESH)
+    pl.semaphore_wait(barrier, 4)
+
+    rows = tok_ref.shape[0]
+    step = rows // pieces
+    dev = x * 2 + s
+    cross = (1 - x) * 2 + s
+    copies = []
+    for g in range(pieces):
+        part_rows = pl.ds(g * step, step)
+        copies.append((
+            pltpu.make_async_remote_copy(
+                tok_ref.at[part_rows], tg.at[part_rows, dev], gb_s.at[g], gb_r.at[g],
+                device_id={"ch": 1 - x}, device_id_type=MESH),
+            pltpu.make_async_remote_copy(
+                tok_ref.at[part_rows], tg.at[part_rows, dev], ga_s.at[g], ga_r.at[g],
+                device_id={"sub": 1 - s}, device_id_type=MESH),
+            pltpu.make_async_remote_copy(
+                tg.at[part_rows, cross], tg.at[part_rows, cross], gf_s.at[g], gf_r.at[g],
+                device_id={"sub": 1 - s}, device_id_type=MESH),
+        ))
+    for over_x, over_s, _ in copies:
+        over_x.start()
+        over_s.start()
+    tg[:, dev] = tok_ref[...]
+    for over_x, _, onward in copies:
+        over_x.wait_recv()
+        onward.start()
+    for over_x, over_s, onward in copies:
+        over_s.wait_recv()
+        onward.wait_recv()
+        over_x.wait_send()
+        over_s.wait_send()
+        onward.wait_send()
+    flat = tg[...].reshape(tt.shape[1], tt.shape[0])
+    tt[...] = jnp.transpose(flat)
+
+    def right_copy(c, d):
+        return pltpu.make_async_remote_copy(
+            s_r.at[c, d], r_r.at[c, d], rs_s.at[c, d], rs_r.at[c, d],
+            device_id={"tok": z + 1}, device_id_type=MESH)
+
+    def left_copy(c, d):
+        return pltpu.make_async_remote_copy(
+            s_l.at[c, d], r_l.at[c, d], ls_s.at[c, d], ls_r.at[c, d],
+            device_id={"tok": z - 1}, device_id_type=MESH)
+
+    def compute(c, carry):
+        w_copy(c).wait()
+        product = jnp.dot(tt[...], wv[c], preferred_element_type=jnp.float32)
+        part[c] = product.reshape(n, ob, hc)
+
+        @pl.when(z == 0)
+        def _():
+            for d in range(n - 1, 0, -1):
+                s_r[c, d] = part[c, d].astype(jnp.bfloat16)
+                right_copy(c, d).start()
+
+        @pl.when(z == n - 1)
+        def _():
+            for d in range(n - 1):
+                s_l[c, d] = part[c, d].astype(jnp.bfloat16)
+                left_copy(c, d).start()
+
+        return carry
+
+    lax.fori_loop(0, chunks, compute, 0)
+
+    def forward(c, carry):
+        for d in range(n - 1, 0, -1):
+            @pl.when((z > 0) & (z < d))
+            def _():
+                right_copy(c, d).wait_recv()
+                s_r[c, d] = (part[c, d] + r_r[c, d].astype(jnp.float32)).astype(jnp.bfloat16)
+                right_copy(c, d).start()
+
+        for d in range(n - 1):
+            @pl.when((z < n - 1) & (z > d))
+            def _():
+                left_copy(c, d).wait_recv()
+                s_l[c, d] = (part[c, d] + r_l[c, d].astype(jnp.float32)).astype(jnp.bfloat16)
+                left_copy(c, d).start()
+
+        for d in range(n):
+            @pl.when(z == d)
+            def _():
+                total = part[c, d]
+                if d > 0:
+                    right_copy(c, d).wait_recv()
+                    total = total + r_r[c, d].astype(jnp.float32)
+                if d < n - 1:
+                    left_copy(c, d).wait_recv()
+                    total = total + r_l[c, d].astype(jnp.float32)
+                out_ref[:, pl.ds(pl.multiple_of(c * hc, hc), hc)] = gelu_exact(total).astype(out_ref.dtype)
+
+        return carry
+
+    lax.fori_loop(0, chunks, forward, 0)
+
+    def drain(c, carry):
+        for d in range(n):
+            @pl.when(z < d)
+            def _():
+                right_copy(c, d).wait_send()
+
+            @pl.when(z > d)
+            def _():
+                left_copy(c, d).wait_send()
+
+        return carry
+
+    lax.fori_loop(0, chunks, drain, 0)
+
+
+def lift(local_tokens, token_mixing):
+    n = lax.axis_size("tok")
+    rows, width, embed = local_tokens.shape
+    depth, cols = token_mixing.shape
+    hc = cols // CHUNKS
+    ob = embed // n
+    dma, bf16 = pltpu.SemaphoreType.DMA, jnp.bfloat16
+    blocks = pltpu.VMEM((CHUNKS, n, ob, hc), bf16)
+    return pl.pallas_call(
+        functools.partial(lift_kernel, n),
+        out_shape=jax.ShapeDtypeStruct((ob, cols), bf16),
+        in_specs=[pl.BlockSpec(memory_space=pltpu.VMEM), pl.BlockSpec(memory_space=pl.ANY)],
+        out_specs=pl.BlockSpec(memory_space=pltpu.VMEM),
+        scratch_shapes=[
+            pltpu.VMEM((rows, 4, width, embed), bf16),
+            pltpu.VMEM((embed, depth), bf16),
+            pltpu.VMEM((CHUNKS, depth, hc), bf16),
+            pltpu.VMEM((CHUNKS, n, ob, hc), jnp.float32),
+            blocks, blocks, blocks, blocks,
+            dma((CHUNKS,)),
+        ] + [dma((PIECES,))] * 6 + [dma((CHUNKS, n))] * 4,
+        compiler_params=pltpu.CompilerParams(
+            collective_id=0, has_side_effects=True, vmem_limit_bytes=60 * 1024 * 1024
+        ),
+    )(local_tokens, token_mixing)
+
+
+def fits(token_mixing, embed):
+    n = lax.axis_size("tok")
+    return (
+        lax.axis_size("ch") == 2
+        and lax.axis_size("sub") == 2
+        and 1 < n <= 8
+        and embed % (16 * n) == 0
+        and token_mixing.shape[1] % (128 * CHUNKS) == 0
+    )
+
+
 def local(weather, conv_first, conv_second, patch_embed, token_mixing):
     widened = padded_2(weather, (("tok", 1),), 2, True)
     padded = padded_2(widened, ((("ch", "sub"), 2),), 2, False)
@@ -55,6 +240,8 @@
     field_two = valid_conv(hidden_one, conv_second)
     field_two = field_two.astype(jnp.bfloat16)
     local_tokens = embed_patches(field_two, patch_embed)
+    if fits(token_mixing, patch_embed.shape[1]):
+        return lift(local_tokens, token_mixing)
     gathered = lax.all_gather(local_tokens, ("ch", "sub"), axis=1, tiled=True)
     tokens = gathered.reshape(-1, gathered.shape[2])
     summed = lax.psum_scatter(

time: 174 us -> 125 us (0.72)
  waiting for transfers between devices: 117 us -> 5.59 us
  Pallas kernels: 0 us -> 93.2 us
  between operations: 13.7 us -> 0.24 us
  blocking collectives: 9.54 us -> 0 us
  other arithmetic: 5.78 us -> 0.55 us
  matrix products: 16.6 us -> 11.8 us
  local copies, waits for them, and re-layouts: 3.67 us -> 6.06 us
    reduce_scatter x1 -> x0, waiting for transfers between devices: 111 us -> none  [local(): lax.psum_scatter(lax.dot_general(tokens, token_mixing, (((0,), (0,)), (()...]
    pallas_call x0 -> x1, Pallas kernels: none -> 93.2 us  [lift(): pl.pallas_call(functools.partial(lift_kernel, n), out_shape=jax.ShapeDtyp...]
    all_gather x1 -> x0, blocking collectives: 9.54 us -> none  [local(): gathered = lax.all_gather(local_tokens, ('ch', 'sub'), axis=1, tiled=True)]
    dot_general x1 -> x0, matrix products: 5.32 us -> none  [local(): lax.dot_general(tokens, token_mixing, (((0,), (0,)), ((), ())), preferred...]
    convert_element_type x1 -> x0, other arithmetic: 5.23 us -> none  [local(): return jax.nn.gelu(summed, approximate=False).astype(jnp.bfloat16)]
    unnamed x23 -> x18, local copies, waits for them, and re-layouts: 2.67 us -> 4.13 us
  transfers between devices with their start and end apart: 5 -> 4, of which waited for: 3 -> 2; matrix products, arithmetic and copies ran while one was open for 1% -> 2% of each run, Pallas kernels for 0% -> 0%
where the time goes in v1:
time: 125 us
  Pallas kernels  93.2 us (75%)
  matrix products  11.8 us (9%)
  starting transfers between devices  7.72 us (6%)
  local copies, waits for them, and re-layouts  6.06 us (5%)
  waiting for transfers between devices  5.59 us (4%)
    pallas_call x1, Pallas kernels, lift(): pl.pallas_call(functools.partial(lift_kernel, n), out_shape=jax.ShapeDtyp...  93.2 us
    dot_general x2, matrix products, valid_conv(): jnp.einsum('toi,tixy->oxy', kernel, stacked, precision=lax.Precision.HIGH...  10.8 us
    ppermute x2, starting transfers between devices, padded_2(): lax.ppermute(lax.slice_in_dim(block, block.shape[dim] - width, None, axis...  4.34 us
    unnamed x18, local copies, waits for them, and re-layouts  4.13 us
    ppermute x2, waiting for transfers between devices, padded_2(): lax.ppermute(lax.slice_in_dim(block, 0, width, axis=dim), axis, backward)  3.65 us
    ppermute x2, starting transfers between devices, padded_2(): lax.ppermute(lax.slice_in_dim(block, 0, width, axis=dim), axis, backward)  3.38 us
  transfers between devices with their start and end apart: 4, of which 2 were waited for; matrix products, arithmetic and copies ran while one was open for 2% of the time, Pallas kernels for 0%

profile of v1, /device:TPU:0, one launch (start us, length us, event | category | flops | bytes accessed | tf_op | source)
XLA Modules:
  0.0 125.1 jit_solution(7052578574531831285)
XLA Ops:
  0.0 0.0 copy-start
  0.0 0.8 fusion.54
  0.8 3.1 %collective-permute-start = (f32[64,2,32]{0,2,1:T(8,128)S(1)}, f32[64,2,32]{0,2,1:T(8,128)S(1)}, u32[]{:S(2)}, u32[]{:S(2)}) collective-permute-start(f32[64,2,32]{0,2,1:T(8,128)S(1)} %get-tuple-element.8), channel_id=1, source_target_pairs={{0,4},{4,8},{8,12},{12,0},{1,5},{5,9},{9,13},{13,1},{2,6},{6,10},{... | collective-permute-start | bytes 49160 | tf_op jit(solution)/shard_map/ppermute | solution.py:22
  3.9 2.1 %collective-permute-start.1 = (f32[64,2,32]{0,2,1:T(8,128)S(1)}, f32[64,2,32]{0,2,1:T(8,128)S(1)}, u32[]{:S(2)}, u32[]{:S(2)}) collective-permute-start(f32[64,2,32]{0,2,1:T(8,128)S(1)} %get-tuple-element.7), channel_id=1, source_target_pairs={{4,0},{8,4},{12,8},{0,12},{5,1},{9,5},{13,9},{1,13},{6,2},{10,6},{... | collective-permute-start | bytes 49160 | tf_op jit(solution)/shard_map/ppermute | solution.py:25
  6.0 1.9 %collective-permute-done = f32[64,2,32]{0,2,1:T(8,128)S(1)} collective-permute-done((f32[64,2,32]{0,2,1:T(8,128)S(1)}, f32[64,2,32]{0,2,1:T(8,128)S(1)}, u32[]{:S(2)}, u32[]{:S(2)}) %collective-permute-start) | collective-permute-done | bytes 16416 | tf_op jit(solution)/shard_map/ppermute | solution.py:22
  7.9 1.1 constant_dynamic-update-slice_fusion.1
  9.0 0.0 collective-permute-done.1
  9.0 1.3 %collective-permute-start.2 = (f32[64,36,2]{0,2,1:T(2,128)S(1)}, f32[64,36,2]{0,2,1:T(2,128)S(1)}, u32[]{:S(2)}, u32[]{:S(2)}) collective-permute-start(f32[64,36,2]{0,2,1:T(2,128)S(1)} %get-tuple-element.6), channel_id=1, source_target_pairs={{0,1},{1,2},{2,3},{4,5},{5,6},{6,7},{8,9},{9,10},{10,11},{12,13},{... | collective-permute-start | bytes 55304 | tf_op jit(solution)/shard_map/ppermute | solution.py:22
  10.4 1.0 reshape.15
  11.4 1.3 %collective-permute-start.3 = (f32[64,36,2]{0,2,1:T(2,128)S(1)}, f32[64,36,2]{0,2,1:T(2,128)S(1)}, u32[]{:S(2)}, u32[]{:S(2)}) collective-permute-start(f32[64,36,2]{0,2,1:T(2,128)S(1)} %get-tuple-element.5), channel_id=1, source_target_pairs={{1,0},{2,1},{3,2},{5,4},{6,5},{7,6},{9,8},{10,9},{11,10},{13,12},{... | collective-permute-start | bytes 55304 | tf_op jit(solution)/shard_map/ppermute | solution.py:25
  12.7 0.0 collective-permute-done.2
  12.7 0.1 fusion.13
  12.8 3.6 %collective-permute-done.3 = f32[64,36,2]{0,2,1:T(2,128)S(1)} collective-permute-done((f32[64,36,2]{0,2,1:T(2,128)S(1)}, f32[64,36,2]{0,2,1:T(2,128)S(1)}, u32[]{:S(2)}, u32[]{:S(2)}) %collective-permute-start.3) | collective-permute-done | bytes 18464 | tf_op jit(solution)/shard_map/ppermute | solution.py:25
  16.4 0.1 pad_maximum_fusion
  16.5 0.1 fusion.23
  16.6 0.1 fusion.7
  16.7 0.1 fusion.10
  16.8 0.1 fusion.22
  16.8 0.1 fusion.4
  16.9 0.1 fusion.21
  17.0 0.1 fusion.19
  17.0 0.1 fusion.18
  17.1 0.0 copy-done
  17.1 6.9 %fusion.16 = f32[64,34,34]{0,2,1:T(8,128)S(1)} fusion(f32[9,64,34,34]{1,3,0,2:T(8,128)S(1)} %fusion.18, pred[34]{0:T(512)(128)(4,1)S(1)} %compare_and_fusion, f32[9,64,64]{2,1,0:T(8,128)S(1)} %copy-done), kind=kOutput, calls=%fused_computation.29 | convolution fusion | flops 516186368 | bytes 3106850 | tf_op jit(solution)/shard_map/toi,tixy->oxy/dot_general | solution.py:41
  24.0 0.0 copy-start.1
  24.0 0.1 fusion.47
  24.0 0.1 fusion.46
  24.1 0.1 fusion.45
  24.2 0.1 fusion.44
  24.3 0.1 fusion.43
  24.3 0.1 fusion.42
  24.4 0.1 fusion.41
  24.5 0.1 fusion.40
  24.5 0.1 fusion.39
  24.6 0.3 copy-done.1
  24.9 3.9 %fusion = bf16[32,32,64]{2,1,0:T(8,128)(2,1)S(1)} fusion(f32[9,64,32,32]{1,3,2,0:T(8,128)S(1)} %fusion.39, f32[9,64,64]{2,1,0:T(8,128)S(1)} %copy-done.1), kind=kOutput, calls=%fused_computation.2 | convolution fusion | flops 453050368 | bytes 2637824 | tf_op jit(solution)/shard_map/toi,tixy->oxy/dot_general | solution.py:41
  28.9 1.0 fusion.1.tok_ref
  29.8 93.2 %shard_map.55 = bf16[96,4096]{1,0:T(8,128)(2,1)} custom-call(bf16[16,16,384]{2,1,0:T(8,128)(2,1)} %fusion.1.tok_ref, bf16[1024,4096]{1,0:T(8,128)(2,1)} %w_ref.1), custom_call_target="tpu_custom_call" | custom-call | tf_op jit(solution)/shard_map/pallas_call | solution.py:200
  123.0 2.1 %copy.46 = bf16[96,4096]{1,0:T(8,128)(2,1)} copy(bf16[96,4096]{1,0:T(8,128)(2,1)} %shard_map.55) | data formatting | bytes 1572864
  (4 shorter events, 0.0 us)
Async XLA Ops:
  0.0 17.1 %copy-start = (f32[9,64,64]{2,1,0:T(8,128)S(1)}, f32[9,64,64]{2,1,0:T(8,128)}, u32[]{:S(2)}) copy-start(f32[9,64,64]{2,1,0:T(8,128)} %param.6) | copy-start | bytes 442372
  0.8 7.1 %collective-permute-start = (f32[64,2,32]{0,2,1:T(8,128)S(1)}, f32[64,2,32]{0,2,1:T(8,128)S(1)}, u32[]{:S(2)}, u32[]{:S(2)}) collective-permute-start(f32[64,2,32]{0,2,1:T(8,128)S(1)} %get-tuple-element.8), channel_id=1, source_target_pairs={{0,4},{4,8},{8,12},{12,0},{1,5},{5,9},{9,13},{13,1},{2,6},{6,10},{... | collective-permute-start | bytes 49160 | tf_op jit(solution)/shard_map/ppermute | solution.py:22
  3.9 5.1 %collective-permute-start.1 = (f32[64,2,32]{0,2,1:T(8,128)S(1)}, f32[64,2,32]{0,2,1:T(8,128)S(1)}, u32[]{:S(2)}, u32[]{:S(2)}) collective-permute-start(f32[64,2,32]{0,2,1:T(8,128)S(1)} %get-tuple-element.7), channel_id=1, source_target_pairs={{4,0},{8,4},{12,8},{0,12},{5,1},{9,5},{13,9},{1,13},{6,2},{10,6},{... | collective-permute-start | bytes 49160 | tf_op jit(solution)/shard_map/ppermute | solution.py:25
  9.0 3.6 %collective-permute-start.2 = (f32[64,36,2]{0,2,1:T(2,128)S(1)}, f32[64,36,2]{0,2,1:T(2,128)S(1)}, u32[]{:S(2)}, u32[]{:S(2)}) collective-permute-start(f32[64,36,2]{0,2,1:T(2,128)S(1)} %get-tuple-element.6), channel_id=1, source_target_pairs={{0,1},{1,2},{2,3},{4,5},{5,6},{6,7},{8,9},{9,10},{10,11},{12,13},{... | collective-permute-start | bytes 55304 | tf_op jit(solution)/shard_map/ppermute | solution.py:22
  11.4 5.1 %collective-permute-start.3 = (f32[64,36,2]{0,2,1:T(2,128)S(1)}, f32[64,36,2]{0,2,1:T(2,128)S(1)}, u32[]{:S(2)}, u32[]{:S(2)}) collective-permute-start(f32[64,36,2]{0,2,1:T(2,128)S(1)} %get-tuple-element.5), channel_id=1, source_target_pairs={{1,0},{2,1},{3,2},{5,4},{6,5},{7,6},{9,8},{10,9},{11,10},{13,12},{... | collective-permute-start | bytes 55304 | tf_op jit(solution)/shard_map/ppermute | solution.py:25
  24.0 1.0 copy-start.1

commit v2 on v1

--- a/solution.py
+++ b/solution.py
@@ -10,6 +10,7 @@
 MESH = pl.DeviceIdType.MESH
 CHUNKS = 8
 PIECES = 2
+LAG = 1
 
 
 def padded_2(block, sides, width, periodic):
@@ -54,43 +55,173 @@
     return 0.5 * v * (1.0 + lax.erf(v * 0.7071067811865476))
 
 
+def split_dot(rows, weights):
+    high = rows.astype(jnp.bfloat16)
+    low = (rows - high.astype(jnp.float32)).astype(jnp.bfloat16)
+    w_high = weights.astype(jnp.bfloat16)
+    w_low = (weights - w_high.astype(jnp.float32)).astype(jnp.bfloat16)
+    dims = (((1,), (1,)), ((), ()))
+    return (
+        lax.dot_general(high, w_high, dims, preferred_element_type=jnp.float32)
+        + lax.dot_general(low, w_high, dims, preferred_element_type=jnp.float32)
+        + lax.dot_general(high, w_low, dims, preferred_element_type=jnp.float32)
+    )
+
+
+def row_conv(source, kt, product, lons, width, chans):
+    count = (lons + 2) * width
+    shifted = [source[pl.ds(s, count), :] for s in range(3)]
+    product[pl.ds(0, count), :] = split_dot(jnp.concatenate(shifted, axis=1), kt)
+    return sum(
+        product[pl.ds(r * width, lons * width), r * chans : (r + 1) * chans] for r in range(3)
+    )
+
+
+def taps(kernel_ref):
+    return jnp.concatenate(
+        [jnp.concatenate([kernel_ref[3 * r + s] for s in range(3)], axis=1) for r in range(3)],
+        axis=0,
+    )
+
+
 def lift_kernel(
-    n, tok_ref, w_ref, out_ref, tg, tt, wv, part, s_r, s_l, r_r, r_l,
-    w_sem, ga_s, ga_r, gb_s, gb_r, gf_s, gf_r, rs_s, rs_r, ls_s, ls_r,
+    n, x_ref, k1_ref, k2_ref, pe_ref, w_ref, out_ref,
+    xp, hp, fp, product, pes, pet, send_lo, send_hi, lat_lo, lat_hi, lon_lo, lon_hi, mine,
+    tg, tt, wv, part, s_r, s_l, r_r, r_l,
+    h_s, h_r, w_sem, ga_s, ga_r, gb_s, gb_r, gf_s, gf_r, rs_s, rs_r, ls_s, ls_r,
 ):
     z, x, s = lax.axis_index("tok"), lax.axis_index("ch"), lax.axis_index("sub")
     chunks, _, ob, hc = s_r.shape
     pieces = ga_s.shape[0]
+    lons, lats, chans = x_ref.shape
+    width = lats + 8
+    dev = x * 2 + s
+    last = 3
 
     def w_copy(c):
         return pltpu.make_async_copy(
             w_ref.at[:, pl.ds(pl.multiple_of(c * hc, hc), hc)], wv.at[c], w_sem.at[c]
         )
 
+    barrier = pltpu.get_barrier_semaphore()
+    up, down = lax.rem(z + 1, n), lax.rem(z + n - 1, n)
+    for plane in (down, z, up):
+        for dx in range(2):
+            for ds in range(2):
+                if plane is z and dx == 0 and ds == 0:
+                    continue
+                pl.semaphore_signal(
+                    barrier, inc=1,
+                    device_id={"tok": plane, "ch": lax.rem(x + dx, 2), "sub": lax.rem(s + ds, 2)},
+                    device_id_type=MESH)
+
     for c in range(chunks):
         w_copy(c).start()
-
-    barrier = pltpu.get_barrier_semaphore()
-    pl.semaphore_signal(barrier, inc=1, device_id={"ch": 1 - x}, device_id_type=MESH)
-    pl.semaphore_signal(barrier, inc=1, device_id={"sub": 1 - s}, device_id_type=MESH)
-
-    for peer in (lax.rem(z + 1, n), lax.rem(z + n - 1, n)):
-        pl.semaphore_signal(barrier, inc=1, device_id={"tok": peer}, device_id_type=MESH)
-    pl.semaphore_wait(barrier, 4)
-
-    rows = tok_ref.shape[0]
-    step = rows // pieces
-    dev = x * 2 + s
+    send_lo[...] = x_ref[:, 0:2, :]
+    send_hi[...] = x_ref[:, lats - 2 : lats, :]
+    pl.semaphore_wait(barrier, 11)
+
+    def halo(k, src, dst, plane, where):
+        return pltpu.make_async_remote_copy(
+            src, dst, h_s.at[k], h_r.at[k],
+            device_id={"tok": plane, "ch": where // 2, "sub": lax.rem(where, 2)},
+            device_id_type=MESH)
+
+    low2, mid, high2 = pl.ds(0, 2), pl.ds(2, lons), pl.ds(lons + 2, 2)
+    first2, last2 = pl.ds(0, 2), pl.ds(lons - 2, 2)
+    lon_halos = (
+        halo(0, x_ref.at[last2], lon_lo, up, dev),
+        halo(1, x_ref.at[first2], lon_hi, down, dev),
+    )
+
+    def to_next():
+        return (
+            halo(2, send_hi.at[last2], lat_lo.at[low2], up, dev + 1),
+            halo(3, send_hi.at[first2], lat_lo.at[high2], down, dev + 1),
+            halo(4, send_hi, lat_lo.at[mid], z, dev + 1),
+        )
+
+    def to_before():
+        return (
+            halo(5, send_lo.at[last2], lat_hi.at[low2], up, dev - 1),
+            halo(6, send_lo.at[first2], lat_hi.at[high2], down, dev - 1),
+            halo(7, send_lo, lat_hi.at[mid], z, dev - 1),
+        )
+
+    for copy in lon_halos:
+        copy.start()
+
+    @pl.when(dev < last)
+    def _():
+        for copy in to_next():
+            copy.start()
+
+    @pl.when(dev > 0)
+    def _():
+        for copy in to_before():
+            copy.start()
+
+    xp[pl.ds(2, lons), pl.ds(2, lats), :] = x_ref[...]
+    kt1 = taps(k1_ref)
+    kt2 = taps(k2_ref)
+    for t in range(pes.shape[0]):
+        columns = pl.ds(t * 128, 128)
+        pes[t] = pe_ref[:, columns].astype(jnp.float32)
+        pet[columns, :] = jnp.transpose(
+            jnp.concatenate([pes[t, pl.ds(j, chans, stride=4), :] for j in (0, 2, 1, 3)], axis=0)
+        ).astype(jnp.bfloat16)
+
+    @pl.when(dev == 0)
+    def _():
+        lat_lo[...] = jnp.zeros_like(lat_lo)
+
+    @pl.when(dev == last)
+    def _():
+        lat_hi[...] = jnp.zeros_like(lat_hi)
+
+    @pl.when(dev > 0)
+    def _():
+        for copy in to_next():
+            copy.wait_recv()
+
+    @pl.when(dev < last)
+    def _():
+        for copy in to_before():
+            copy.wait_recv()
+
+    for copy in lon_halos:
+        copy.wait_recv()
+
+    xp[pl.ds(0, 2), pl.ds(2, lats), :] = lon_lo[...]
+    xp[pl.ds(lons + 2, 2), pl.ds(2, lats), :] = lon_hi[...]
+    xp[pl.ds(0, lons + 4), pl.ds(0, 2), :] = lat_lo[...]
+    xp[pl.ds(0, lons + 4), pl.ds(lats + 2, 2), :] = lat_hi[...]
+
+    flat_x = xp.reshape((lons + 5) * width, chans)
+    hidden = gelu_exact(row_conv(flat_x, kt1, product, lons + 2, width, chans))
+    lat = lax.broadcasted_iota(jnp.int32, (lons + 2, width, chans), 1) + (dev * lats - 1)
+    hidden = hidden.reshape(lons + 2, width, chans)
+    hidden = jnp.where((lat >= 0) & (lat < 4 * lats), hidden, 0.0)
+    hp[pl.ds(0, (lons + 2) * width), :] = hidden.reshape((lons + 2) * width, chans)
+    field = row_conv(hp, kt2, product, lons, width, chans)
+    field = field.astype(jnp.bfloat16).astype(jnp.float32)
+    field = field.reshape(lons // 2, 2, width, chans)
+    fp[...] = jnp.concatenate([field[:, 0], field[:, 1]], axis=2)
+    mine[...] = jnp.concatenate(
+        [fp[:, pl.ds(b, lats // 2, stride=2), :] for b in range(2)], axis=2
+    ).astype(jnp.bfloat16)
+
+    step = mine.shape[0] // pieces
     cross = (1 - x) * 2 + s
     copies = []
     for g in range(pieces):
         part_rows = pl.ds(g * step, step)
         copies.append((
             pltpu.make_async_remote_copy(
-                tok_ref.at[part_rows], tg.at[part_rows, dev], gb_s.at[g], gb_r.at[g],
+                mine.at[part_rows], tg.at[part_rows, dev], gb_s.at[g], gb_r.at[g],
                 device_id={"ch": 1 - x}, device_id_type=MESH),
             pltpu.make_async_remote_copy(
-                tok_ref.at[part_rows], tg.at[part_rows, dev], ga_s.at[g], ga_r.at[g],
+                mine.at[part_rows], tg.at[part_rows, dev], ga_s.at[g], ga_r.at[g],
                 device_id={"sub": 1 - s}, device_id_type=MESH),
             pltpu.make_async_remote_copy(
                 tg.at[part_rows, cross], tg.at[part_rows, cross], gf_s.at[g], gf_r.at[g],
@@ -99,7 +230,7 @@
     for over_x, over_s, _ in copies:
         over_x.start()
         over_s.start()
-    tg[:, dev] = tok_ref[...]
+    tg[:, dev] = mine[...]
     for over_x, _, onward in copies:
         over_x.wait_recv()
         onward.start()
@@ -109,8 +240,23 @@
         over_x.wait_send()
         over_s.wait_send()
         onward.wait_send()
-    flat = tg[...].reshape(tt.shape[1], tt.shape[0])
-    tt[...] = jnp.transpose(flat)
+    for copy in lon_halos:
+        copy.wait_send()
+
+    @pl.when(dev < last)
+    def _():
+        for copy in to_next():
+            copy.wait_send()
+
+    @pl.when(dev > 0)
+    def _():
+        for copy in to_before():
+            copy.wait_send()
+
+    flat = tg[...].reshape(tt.shape[1], pet.shape[1])
+    tt[...] = lax.dot_general(
+        pet[...], flat, (((1,), (1,)), ((), ())), preferred_element_type=jnp.float32
+    ).astype(jnp.bfloat16)
 
     def right_copy(c, d):
         return pltpu.make_async_remote_copy(
@@ -143,36 +289,41 @@
 
     lax.fori_loop(0, chunks, compute, 0)
 
-    def forward(c, carry):
+    right_lag = jnp.maximum(z - 1, 0) * LAG
+    left_lag = jnp.maximum(n - 2 - z, 0) * LAG
+    last_lag = jnp.maximum(right_lag, left_lag)
+
+    def forward(i, carry):
+        c_r, c_l, c_o = i - right_lag, i - left_lag, i - last_lag
         for d in range(n - 1, 0, -1):
-            @pl.when((z > 0) & (z < d))
+            @pl.when((z > 0) & (z < d) & (c_r >= 0) & (c_r < chunks))
             def _():
-                right_copy(c, d).wait_recv()
-                s_r[c, d] = (part[c, d] + r_r[c, d].astype(jnp.float32)).astype(jnp.bfloat16)
-                right_copy(c, d).start()
+                right_copy(c_r, d).wait_recv()
+                s_r[c_r, d] = (part[c_r, d] + r_r[c_r, d].astype(jnp.float32)).astype(jnp.bfloat16)
+                right_copy(c_r, d).start()
 
         for d in range(n - 1):
-            @pl.when((z < n - 1) & (z > d))
+            @pl.when((z < n - 1) & (z > d) & (c_l >= 0) & (c_l < chunks))
             def _():
-                left_copy(c, d).wait_recv()
-                s_l[c, d] = (part[c, d] + r_l[c, d].astype(jnp.float32)).astype(jnp.bfloat16)
-                left_copy(c, d).start()
+                left_copy(c_l, d).wait_recv()
+                s_l[c_l, d] = (part[c_l, d] + r_l[c_l, d].astype(jnp.float32)).astype(jnp.bfloat16)
+                left_copy(c_l, d).start()
 
         for d in range(n):
-            @pl.when(z == d)
+            @pl.when((z == d) & (c_o >= 0) & (c_o < chunks))
             def _():
-                total = part[c, d]
+                total = part[c_o, d]
                 if d > 0:
-                    right_copy(c, d).wait_recv()
-                    total = total + r_r[c, d].astype(jnp.float32)
+                    right_copy(c_o, d).wait_recv()
+                    total = total + r_r[c_o, d].astype(jnp.float32)
                 if d < n - 1:
-                    left_copy(c, d).wait_recv()
-                    total = total + r_l[c, d].astype(jnp.float32)
-                out_ref[:, pl.ds(pl.multiple_of(c * hc, hc), hc)] = gelu_exact(total).astype(out_ref.dtype)
+                    left_copy(c_o, d).wait_recv()
+                    total = total + r_l[c_o, d].astype(jnp.float32)
+                out_ref[:, pl.ds(pl.multiple_of(c_o * hc, hc), hc)] = gelu_exact(total).astype(out_ref.dtype)
 
         return carry
 
-    lax.fori_loop(0, chunks, forward, 0)
+    lax.fori_loop(0, chunks + (n - 2) * LAG, forward, 0)
 
     def drain(c, carry):
         for d in range(n):
@@ -189,45 +340,68 @@
     lax.fori_loop(0, chunks, drain, 0)
 
 
-def lift(local_tokens, token_mixing):
+def lift(turned, conv_first, conv_second, patch_embed, token_mixing):
     n = lax.axis_size("tok")
-    rows, width, embed = local_tokens.shape
+    lons, lats, chans = turned.shape
+    embed = patch_embed.shape[1]
     depth, cols = token_mixing.shape
     hc = cols // CHUNKS
     ob = embed // n
-    dma, bf16 = pltpu.SemaphoreType.DMA, jnp.bfloat16
+    width = lats + 8
+    dma, bf16, f32 = pltpu.SemaphoreType.DMA, jnp.bfloat16, jnp.float32
     blocks = pltpu.VMEM((CHUNKS, n, ob, hc), bf16)
+    held = pl.BlockSpec(memory_space=pltpu.VMEM)
     return pl.pallas_call(
         functools.partial(lift_kernel, n),
         out_shape=jax.ShapeDtypeStruct((ob, cols), bf16),
-        in_specs=[pl.BlockSpec(memory_space=pltpu.VMEM), pl.BlockSpec(memory_space=pl.ANY)],
-        out_specs=pl.BlockSpec(memory_space=pltpu.VMEM),
+        in_specs=[held, held, held, held, pl.BlockSpec(memory_space=pl.ANY)],
+        out_specs=held,
         scratch_shapes=[
-            pltpu.VMEM((rows, 4, width, embed), bf16),
+            pltpu.VMEM((lons + 5, width, chans), f32),
+            pltpu.VMEM(((lons + 3) * width, chans), f32),
+            pltpu.VMEM((lons // 2, width, 2 * chans), f32),
+            pltpu.VMEM(((lons + 4) * width, 3 * chans), f32),
+            pltpu.VMEM((embed // 128, 4 * chans, 128), f32),
+            pltpu.VMEM((embed, 4 * chans), bf16),
+            pltpu.VMEM((lons, 2, chans), f32),
+            pltpu.VMEM((lons, 2, chans), f32),
+            pltpu.VMEM((lons + 4, 2, chans), f32),
+            pltpu.VMEM((lons + 4, 2, chans), f32),
+            pltpu.VMEM((2, lats, chans), f32),
+            pltpu.VMEM((2, lats, chans), f32),
+            pltpu.VMEM((lons // 2, lats // 2, 4 * chans), bf16),
+            pltpu.VMEM((lons // 2, 4, lats // 2, 4 * chans), bf16),
             pltpu.VMEM((embed, depth), bf16),
             pltpu.VMEM((CHUNKS, depth, hc), bf16),
-            pltpu.VMEM((CHUNKS, n, ob, hc), jnp.float32),
+            pltpu.VMEM((CHUNKS, n, ob, hc), f32),
             blocks, blocks, blocks, blocks,
-            dma((CHUNKS,)),
+            dma((8,)), dma((8,)), dma((CHUNKS,)),
         ] + [dma((PIECES,))] * 6 + [dma((CHUNKS, n))] * 4,
         compiler_params=pltpu.CompilerParams(
             collective_id=0, has_side_effects=True, vmem_limit_bytes=60 * 1024 * 1024
         ),
-    )(local_tokens, token_mixing)
-
-
-def fits(token_mixing, embed):
+    )(turned, conv_first, conv_second, patch_embed, token_mixing)
+
+
+def fits(weather, token_mixing, embed):
     n = lax.axis_size("tok")
     return (
         lax.axis_size("ch") == 2
         and lax.axis_size("sub") == 2
-        and 1 < n <= 8
+        and 2 < n <= 8
         and embed % (16 * n) == 0
         and token_mixing.shape[1] % (128 * CHUNKS) == 0
+        and weather.shape[1] % (4 * PIECES) == 0
+        and weather.shape[2] % 32 == 0
+        and 2 * weather.shape[0] == 128
+        and embed % 128 == 0
     )
 
 
 def local(weather, conv_first, conv_second, patch_embed, token_mixing):
+    if fits(weather, token_mixing, patch_embed.shape[1]):
+        turned = jnp.transpose(weather, (1, 2, 0))
+        return lift(turned, conv_first, conv_second, patch_embed, token_mixing)
     widened = padded_2(weather, (("tok", 1),), 2, True)
     padded = padded_2(widened, ((("ch", "sub"), 2),), 2, False)
     hidden_one = jax.nn.gelu(valid_conv(padded, conv_first), approximate=False)
@@ -240,8 +414,6 @@
     field_two = valid_conv(hidden_one, conv_second)
     field_two = field_two.astype(jnp.bfloat16)
     local_tokens = embed_patches(field_two, patch_embed)
-    if fits(token_mixing, patch_embed.shape[1]):
-        return lift(local_tokens, token_mixing)
     gathered = lax.all_gather(local_tokens, ("ch", "sub"), axis=1, tiled=True)
     tokens = gathered.reshape(-1, gathered.shape[2])
     summed = lax.psum_scatter(

time: 125 us -> 81.9 us (0.66)
  Pallas kernels: 93.2 us -> 79.6 us
  matrix products: 11.8 us -> 0 us
  starting transfers between devices: 7.72 us -> 0 us
  waiting for transfers between devices: 5.59 us -> 0 us
  local copies, waits for them, and re-layouts: 6.06 us -> 2.06 us
    pallas_call x1, Pallas kernels: 93.2 us -> 79.6 us  [lift(): pl.pallas_call(functools.partial(lift_kernel, n), out_shape=jax.ShapeDtyp...]
    dot_general x3 -> x0, matrix products: 11.8 us -> none  [the longest x2 10.8 us: valid_conv(): jnp.einsum('toi,tixy->oxy', kernel, stacked, precision=lax.Precision.HIGH...]
    ppermute x4 -> x0, starting transfers between devices: 7.72 us -> none  [the longest x2 4.34 us: padded_2(): lax.ppermute(lax.slice_in_dim(block, block.shape[dim] - width, None, axis...]
    ppermute x4 -> x0, waiting for transfers between devices: 5.59 us -> none  [the longest x2 3.65 us: padded_2(): lax.ppermute(lax.slice_in_dim(block, 0, width, axis=dim), axis, backward)]
    unnamed x18 -> x1, local copies, waits for them, and re-layouts: 4.13 us -> 2.06 us
  transfers between devices with their start and end apart: 4 -> 0, of which waited for: 2 -> 0; matrix products, arithmetic and copies ran while one was open for 2% -> 0% of each run, Pallas kernels for 0% -> 0%
where the time goes in v2:
time: 81.9 us; the launch traced here: 81.7 us
  Pallas kernels  79.6 us (97%)
  local copies, waits for them, and re-layouts  2.06 us (3%)
    pallas_call x1, Pallas kernels, lift(): pl.pallas_call(functools.partial(lift_kernel, n), out_shape=jax.ShapeDtyp...  79.6 us
    unnamed x1, local copies, waits for them, and re-layouts  2.06 us

profile of v2, /device:TPU:0, one launch (start us, length us, event | category | flops | bytes accessed | tf_op | source)
XLA Modules:
  0.0 81.7 jit_solution(7320301844681464082)
XLA Ops:
  0.0 79.6 %shard_map.55 = bf16[96,4096]{1,0:T(8,128)(2,1)} custom-call(f32[32,32,64]{2,1,0:T(8,128)} %bitcast.1, f32[9,64,64]{2,1,0:T(8,128)} %k1_ref.1, f32[9,64,64]{2,1,0:T(8,128)} %k2_ref.1, bf16[256,384]{1,0:T(8,128)(2,1)} %pe_ref.1, bf16[1024,4096]{1,0:T(8,128)(2,1)} %w_ref.1), custom_call_target="tpu_custom_call" | custom-call | tf_op jit(solution)/shard_map/pallas_call | solution.py:354
  79.6 2.1 %copy.7 = bf16[96,4096]{1,0:T(8,128)(2,1)} copy(bf16[96,4096]{1,0:T(8,128)(2,1)} %shard_map.55) | data formatting | bytes 1572864

commit v3 on v2

--- a/solution.py
+++ b/solution.py
@@ -8,9 +8,10 @@
 from jax.sharding import PartitionSpec as P
 
 MESH = pl.DeviceIdType.MESH
-CHUNKS = 8
+CHUNKS = 4
 PIECES = 2
 LAG = 1
+DELAY = 1
 
 
 def padded_2(block, sides, width, periodic):
@@ -68,9 +69,9 @@
     )
 
 
-def row_conv(source, kt, product, lons, width, chans):
+def row_conv(source, kt, product, first, lons, width, chans):
     count = (lons + 2) * width
-    shifted = [source[pl.ds(s, count), :] for s in range(3)]
+    shifted = [source[pl.ds(first * width + s, count), :] for s in range(3)]
     product[pl.ds(0, count), :] = split_dot(jnp.concatenate(shifted, axis=1), kt)
     return sum(
         product[pl.ds(r * width, lons * width), r * chans : (r + 1) * chans] for r in range(3)
@@ -85,15 +86,16 @@
 
 
 def lift_kernel(
-    n, x_ref, k1_ref, k2_ref, pe_ref, w_ref, out_ref,
+    n, x_in, k1_in, k2_in, pe_in, w_ref, out_ref,
+    x_ref, k1_ref, k2_ref, pe_ref,
     xp, hp, fp, product, pes, pet, send_lo, send_hi, lat_lo, lat_hi, lon_lo, lon_hi, mine,
     tg, tt, wv, part, s_r, s_l, r_r, r_l,
-    h_s, h_r, w_sem, ga_s, ga_r, gb_s, gb_r, gf_s, gf_r, rs_s, rs_r, ls_s, ls_r,
+    in_sem, h_s, h_r, w_sem, ga_s, ga_r, gb_s, gb_r, gf_s, gf_r, rs_s, rs_r, ls_s, ls_r,
 ):
     z, x, s = lax.axis_index("tok"), lax.axis_index("ch"), lax.axis_index("sub")
     chunks, _, ob, hc = s_r.shape
     pieces = ga_s.shape[0]
-    lons, lats, chans = x_ref.shape
+    lons, lats, chans = x_in.shape
     width = lats + 8
     dev = x * 2 + s
     last = 3
@@ -103,6 +105,13 @@
             w_ref.at[:, pl.ds(pl.multiple_of(c * hc, hc), hc)], wv.at[c], w_sem.at[c]
         )
 
+    fetches = [
+        pltpu.make_async_copy(src, dst, in_sem.at[k])
+        for k, (src, dst) in enumerate(
+            ((x_in, x_ref), (k1_in, k1_ref), (k2_in, k2_ref), (pe_in, pe_ref))
+        )
+    ]
+    fetches[0].start()
     barrier = pltpu.get_barrier_semaphore()
     up, down = lax.rem(z + 1, n), lax.rem(z + n - 1, n)
     for plane in (down, z, up):
@@ -115,8 +124,11 @@
                     device_id={"tok": plane, "ch": lax.rem(x + dx, 2), "sub": lax.rem(s + ds, 2)},
                     device_id_type=MESH)
 
+    for copy in fetches[1:]:
+        copy.start()
     for c in range(chunks):
         w_copy(c).start()
+    fetches[0].wait()
     send_lo[...] = x_ref[:, 0:2, :]
     send_hi[...] = x_ref[:, lats - 2 : lats, :]
     pl.semaphore_wait(barrier, 11)
@@ -162,6 +174,8 @@
             copy.start()
 
     xp[pl.ds(2, lons), pl.ds(2, lats), :] = x_ref[...]
+    for copy in fetches[1:]:
+        copy.wait()
     kt1 = taps(k1_ref)
     kt2 = taps(k2_ref)
     for t in range(pes.shape[0]):
@@ -181,35 +195,45 @@
 
     @pl.when(dev > 0)
     def _():
-        for copy in to_next():
+        to_next()[2].wait_recv()
+
+    @pl.when(dev < last)
+    def _():
+        to_before()[2].wait_recv()
+
+    xp[mid, pl.ds(0, 2), :] = lat_lo[mid]
+    xp[mid, pl.ds(lats + 2, 2), :] = lat_hi[mid]
+    flat_x = xp.reshape((lons + 5) * width, chans)
+
+    def hide(first, count):
+        hidden = gelu_exact(row_conv(flat_x, kt1, product, first, count, width, chans))
+        lat = lax.broadcasted_iota(jnp.int32, (count, width, chans), 1) + (dev * lats - 1)
+        hidden = hidden.reshape(count, width, chans)
+        hidden = jnp.where((lat >= 0) & (lat < 4 * lats), hidden, 0.0)
+        hp[pl.ds(first * width, count * width), :] = hidden.reshape(count * width, chans)
+
+    hide(2, lons - 2)
+
+    @pl.when(dev > 0)
+    def _():
+        for copy in to_next()[:2]:
             copy.wait_recv()
 
     @pl.when(dev < last)
     def _():
-        for copy in to_before():
+        for copy in to_before()[:2]:
             copy.wait_recv()
 
     for copy in lon_halos:
         copy.wait_recv()
 
-    xp[pl.ds(0, 2), pl.ds(2, lats), :] = lon_lo[...]
-    xp[pl.ds(lons + 2, 2), pl.ds(2, lats), :] = lon_hi[...]
-    xp[pl.ds(0, lons + 4), pl.ds(0, 2), :] = lat_lo[...]
-    xp[pl.ds(0, lons + 4), pl.ds(lats + 2, 2), :] = lat_hi[...]
-
-    flat_x = xp.reshape((lons + 5) * width, chans)
-    hidden = gelu_exact(row_conv(flat_x, kt1, product, lons + 2, width, chans))
-    lat = lax.broadcasted_iota(jnp.int32, (lons + 2, width, chans), 1) + (dev * lats - 1)
-    hidden = hidden.reshape(lons + 2, width, chans)
-    hidden = jnp.where((lat >= 0) & (lat < 4 * lats), hidden, 0.0)
-    hp[pl.ds(0, (lons + 2) * width), :] = hidden.reshape((lons + 2) * width, chans)
-    field = row_conv(hp, kt2, product, lons, width, chans)
-    field = field.astype(jnp.bfloat16).astype(jnp.float32)
-    field = field.reshape(lons // 2, 2, width, chans)
-    fp[...] = jnp.concatenate([field[:, 0], field[:, 1]], axis=2)
-    mine[...] = jnp.concatenate(
-        [fp[:, pl.ds(b, lats // 2, stride=2), :] for b in range(2)], axis=2
-    ).astype(jnp.bfloat16)
+    xp[low2, pl.ds(2, lats), :] = lon_lo[...]
+    xp[high2, pl.ds(2, lats), :] = lon_hi[...]
+    for side in (low2, high2):
+        xp[side, pl.ds(0, 2), :] = lat_lo[side]
+        xp[side, pl.ds(lats + 2, 2), :] = lat_hi[side]
+    hide(0, 2)
+    hide(lons, 2)
 
     step = mine.shape[0] // pieces
     cross = (1 - x) * 2 + s
@@ -227,7 +251,15 @@
                 tg.at[part_rows, cross], tg.at[part_rows, cross], gf_s.at[g], gf_r.at[g],
                 device_id={"sub": 1 - s}, device_id_type=MESH),
         ))
-    for over_x, over_s, _ in copies:
+    for g, (over_x, over_s, _) in enumerate(copies):
+        count = 2 * step
+        field = row_conv(hp, kt2, product, g * count, count, width, chans)
+        field = field.astype(jnp.bfloat16).astype(jnp.float32)
+        field = field.reshape(step, 2, width, chans)
+        fp[...] = jnp.concatenate([field[:, 0], field[:, 1]], axis=2)
+        mine[pl.ds(g * step, step)] = jnp.concatenate(
+            [fp[:, pl.ds(b, lats // 2, stride=2), :] for b in range(2)], axis=2
+        ).astype(jnp.bfloat16)
         over_x.start()
         over_s.start()
     tg[:, dev] = mine[...]
@@ -268,34 +300,44 @@
             s_l.at[c, d], r_l.at[c, d], ls_s.at[c, d], ls_r.at[c, d],
             device_id={"tok": z - 1}, device_id_type=MESH)
 
+    def sources(i):
+        for d in range(n - 1, 0, -1):
+            c = i - (n - 1 - d) * DELAY
+
+            @pl.when((z == 0) & (c >= 0) & (c < chunks))
+            def _():
+                s_r[c, d] = part[c, d].astype(jnp.bfloat16)
+                right_copy(c, d).start()
+
+        for d in range(n - 1):
+            c = i - d * DELAY
+
+            @pl.when((z == n - 1) & (c >= 0) & (c < chunks))
+            def _():
+                s_l[c, d] = part[c, d].astype(jnp.bfloat16)
+                left_copy(c, d).start()
+
     def compute(c, carry):
         w_copy(c).wait()
         product = jnp.dot(tt[...], wv[c], preferred_element_type=jnp.float32)
         part[c] = product.reshape(n, ob, hc)
 
-        @pl.when(z == 0)
-        def _():
-            for d in range(n - 1, 0, -1):
-                s_r[c, d] = part[c, d].astype(jnp.bfloat16)
-                right_copy(c, d).start()
-
-        @pl.when(z == n - 1)
-        def _():
-            for d in range(n - 1):
-                s_l[c, d] = part[c, d].astype(jnp.bfloat16)
-                left_copy(c, d).start()
-
+        sources(c)
         return carry
 
     lax.fori_loop(0, chunks, compute, 0)
+    for late in range((n - 2) * DELAY):
+        sources(chunks + late)
 
     right_lag = jnp.maximum(z - 1, 0) * LAG
     left_lag = jnp.maximum(n - 2 - z, 0) * LAG
-    last_lag = jnp.maximum(right_lag, left_lag)
+    last_lag = jnp.maximum(right_lag + (n - 1 - z) * DELAY, left_lag + z * DELAY)
 
     def forward(i, carry):
-        c_r, c_l, c_o = i - right_lag, i - left_lag, i - last_lag
+        c_o = i - last_lag
         for d in range(n - 1, 0, -1):
+            c_r = i - right_lag - (n - 1 - d) * DELAY
+
             @pl.when((z > 0) & (z < d) & (c_r >= 0) & (c_r < chunks))
             def _():
                 right_copy(c_r, d).wait_recv()
@@ -303,6 +345,8 @@
                 right_copy(c_r, d).start()
 
         for d in range(n - 1):
+            c_l = i - left_lag - d * DELAY
+
             @pl.when((z < n - 1) & (z > d) & (c_l >= 0) & (c_l < chunks))
             def _():
                 left_copy(c_l, d).wait_recv()
@@ -323,7 +367,7 @@
 
         return carry
 
-    lax.fori_loop(0, chunks + (n - 2) * LAG, forward, 0)
+    lax.fori_loop(0, chunks + (n - 1) * DELAY + (n - 2) * LAG, forward, 0)
 
     def drain(c, carry):
         for d in range(n):
@@ -354,12 +398,16 @@
     return pl.pallas_call(
         functools.partial(lift_kernel, n),
         out_shape=jax.ShapeDtypeStruct((ob, cols), bf16),
-        in_specs=[held, held, held, held, pl.BlockSpec(memory_space=pl.ANY)],
+        in_specs=[pl.BlockSpec(memory_space=pl.ANY)] * 5,
         out_specs=held,
         scratch_shapes=[
+            pltpu.VMEM(turned.shape, f32),
+            pltpu.VMEM(conv_first.shape, f32),
+            pltpu.VMEM(conv_second.shape, f32),
+            pltpu.VMEM(patch_embed.shape, bf16),
             pltpu.VMEM((lons + 5, width, chans), f32),
             pltpu.VMEM(((lons + 3) * width, chans), f32),
-            pltpu.VMEM((lons // 2, width, 2 * chans), f32),
+            pltpu.VMEM((lons // 2 // PIECES, width, 2 * chans), f32),
             pltpu.VMEM(((lons + 4) * width, 3 * chans), f32),
             pltpu.VMEM((embed // 128, 4 * chans, 128), f32),
             pltpu.VMEM((embed, 4 * chans), bf16),
@@ -375,7 +423,7 @@
             pltpu.VMEM((CHUNKS, depth, hc), bf16),
             pltpu.VMEM((CHUNKS, n, ob, hc), f32),
             blocks, blocks, blocks, blocks,
-            dma((8,)), dma((8,)), dma((CHUNKS,)),
+            dma((4,)), dma((8,)), dma((8,)), dma((CHUNKS,)),
         ] + [dma((PIECES,))] * 6 + [dma((CHUNKS, n))] * 4,
         compiler_params=pltpu.CompilerParams(
             collective_id=0, has_side_effects=True, vmem_limit_bytes=60 * 1024 * 1024

time: 81.9 us -> 73.4 us (0.90)
  Pallas kernels: 79.6 us -> 70.7 us
    pallas_call x1, Pallas kernels: 79.6 us -> 70.7 us  [lift(): pl.pallas_call(functools.partial(lift_kernel, n), out_shape=jax.ShapeDtyp...]
where the time goes in v3:
time: 73.4 us; the launch traced here: 72.8 us
  Pallas kernels  70.7 us (96%)
  local copies, waits for them, and re-layouts  2.06 us (3%)
    pallas_call x1, Pallas kernels, lift(): pl.pallas_call(functools.partial(lift_kernel, n), out_shape=jax.ShapeDtyp...  70.7 us
    unnamed x1, local copies, waits for them, and re-layouts  2.06 us

profile of v3, /device:TPU:0, one launch (start us, length us, event | category | flops | bytes accessed | tf_op | source)
XLA Modules:
  0.0 72.8 jit_solution(14398982163765457977)
XLA Ops:
  0.0 70.7 %shard_map.55 = bf16[96,4096]{1,0:T(8,128)(2,1)} custom-call(f32[32,32,64]{2,1,0:T(8,128)} %bitcast.1, f32[9,64,64]{2,1,0:T(8,128)} %k1_in.1, f32[9,64,64]{2,1,0:T(8,128)} %k2_in.1, bf16[256,384]{1,0:T(8,128)(2,1)} %pe_in.1, bf16[1024,4096]{1,0:T(8,128)(2,1)} %w_ref.1), custom_call_target="tpu_custom_call" | custom-call | tf_op jit(solution)/shard_map/pallas_call | solution.py:398
  70.7 2.1 %copy.7 = bf16[96,4096]{1,0:T(8,128)(2,1)} copy(bf16[96,4096]{1,0:T(8,128)(2,1)} %shard_map.55) | data formatting | bytes 1572864

commit v4 on v3

--- a/solution.py
+++ b/solution.py
@@ -89,8 +89,8 @@
     n, x_in, k1_in, k2_in, pe_in, w_ref, out_ref,
     x_ref, k1_ref, k2_ref, pe_ref,
     xp, hp, fp, product, pes, pet, send_lo, send_hi, lat_lo, lat_hi, lon_lo, lon_hi, mine,
-    tg, tt, wv, part, s_r, s_l, r_r, r_l,
-    in_sem, h_s, h_r, w_sem, ga_s, ga_r, gb_s, gb_r, gf_s, gf_r, rs_s, rs_r, ls_s, ls_r,
+    tg, tt, wv, done, part, s_r, s_l, r_r, r_l,
+    in_sem, h_s, h_r, w_sem, o_sem, ga_s, ga_r, gb_s, gb_r, gf_s, gf_r, rs_s, rs_r, ls_s, ls_r,
 ):
     z, x, s = lax.axis_index("tok"), lax.axis_index("ch"), lax.axis_index("sub")
     chunks, _, ob, hc = s_r.shape
@@ -300,6 +300,11 @@
             s_l.at[c, d], r_l.at[c, d], ls_s.at[c, d], ls_r.at[c, d],
             device_id={"tok": z - 1}, device_id_type=MESH)
 
+    def out_copy(c):
+        return pltpu.make_async_copy(
+            done.at[c], out_ref.at[:, pl.ds(pl.multiple_of(c * hc, hc), hc)], o_sem.at[c]
+        )
+
     def sources(i):
         for d in range(n - 1, 0, -1):
             c = i - (n - 1 - d) * DELAY
@@ -363,13 +368,15 @@
                 if d < n - 1:
                     left_copy(c_o, d).wait_recv()
                     total = total + r_l[c_o, d].astype(jnp.float32)
-                out_ref[:, pl.ds(pl.multiple_of(c_o * hc, hc), hc)] = gelu_exact(total).astype(out_ref.dtype)
+                done[c_o] = gelu_exact(total).astype(done.dtype)
+                out_copy(c_o).start()
 
         return carry
 
     lax.fori_loop(0, chunks + (n - 1) * DELAY + (n - 2) * LAG, forward, 0)
 
     def drain(c, carry):
+        out_copy(c).wait()
         for d in range(n):
             @pl.when(z < d)
             def _():
@@ -394,12 +401,11 @@
     width = lats + 8
     dma, bf16, f32 = pltpu.SemaphoreType.DMA, jnp.bfloat16, jnp.float32
     blocks = pltpu.VMEM((CHUNKS, n, ob, hc), bf16)
-    held = pl.BlockSpec(memory_space=pltpu.VMEM)
     return pl.pallas_call(
         functools.partial(lift_kernel, n),
         out_shape=jax.ShapeDtypeStruct((ob, cols), bf16),
         in_specs=[pl.BlockSpec(memory_space=pl.ANY)] * 5,
-        out_specs=held,
+        out_specs=pl.BlockSpec(memory_space=pl.ANY),
         scratch_shapes=[
             pltpu.VMEM(turned.shape, f32),
             pltpu.VMEM(conv_first.shape, f32),
@@ -421,9 +427,10 @@
             pltpu.VMEM((lons // 2, 4, lats // 2, 4 * chans), bf16),
             pltpu.VMEM((embed, depth), bf16),
             pltpu.VMEM((CHUNKS, depth, hc), bf16),
+            pltpu.VMEM((CHUNKS, ob, hc), bf16),
             pltpu.VMEM((CHUNKS, n, ob, hc), f32),
             blocks, blocks, blocks, blocks,
-            dma((4,)), dma((8,)), dma((8,)), dma((CHUNKS,)),
+            dma((4,)), dma((8,)), dma((8,)), dma((CHUNKS,)), dma((CHUNKS,)),
         ] + [dma((PIECES,))] * 6 + [dma((CHUNKS, n))] * 4,
         compiler_params=pltpu.CompilerParams(
             collective_id=0, has_side_effects=True, vmem_limit_bytes=60 * 1024 * 1024

time: 73.4 us -> 72.9 us (level)
  Pallas kernels: 70.7 us -> 69.9 us
    pallas_call x1, Pallas kernels: 70.7 us -> 69.9 us  [lift(): pl.pallas_call(functools.partial(lift_kernel, n), out_shape=jax.ShapeDtyp...]
where the time goes in v4:
time: 72.9 us; the launch traced here: 72 us
  Pallas kernels  69.9 us (96%)
  local copies, waits for them, and re-layouts  2.06 us (3%)
    pallas_call x1, Pallas kernels, lift(): pl.pallas_call(functools.partial(lift_kernel, n), out_shape=jax.ShapeDtyp...  69.9 us
    unnamed x1, local copies, waits for them, and re-layouts  2.06 us

profile of v4, /device:TPU:0, one launch (start us, length us, event | category | flops | bytes accessed | tf_op | source)
XLA Modules:
  0.0 72.0 jit_solution(8765830290000822250)
XLA Ops:
  0.0 69.9 %shard_map.55 = bf16[96,4096]{1,0:T(8,128)(2,1)} custom-call(f32[32,32,64]{2,1,0:T(8,128)} %bitcast.1, f32[9,64,64]{2,1,0:T(8,128)} %k1_in.1, f32[9,64,64]{2,1,0:T(8,128)} %k2_in.1, bf16[256,384]{1,0:T(8,128)(2,1)} %pe_in.1, bf16[1024,4096]{1,0:T(8,128)(2,1)} %w_ref.1), custom_call_target="tpu_custom_call" | custom-call | tf_op jit(solution)/shard_map/pallas_call | solution.py:404
  69.9 2.1 %copy.7 = bf16[96,4096]{1,0:T(8,128)(2,1)} copy(bf16[96,4096]{1,0:T(8,128)(2,1)} %shard_map.55) | data formatting | bytes 1572864
